TPU v7x, 128 devices: a whole 4x4x4 slice. The times are simulated.
128 devices in a mesh: tab: 32 (over x, y, core), rep: 4 (over z).
Axes of the slice: x: 4, y: 4, z: 4, core: 2. Of those that a mesh axis runs over, the one named last changes fastest.
Arguments:
- pooled: bfloat16 [64, 16384, 128], P('tab', 'rep'), may hold values from -6 to 6
- widths: int32 [64], replicated, may hold values from 16 to 128, as said below
- placement: int32 [64], replicated, may hold values from 0 to 63, each once
- route: int32 [4, 4096], P('rep'), may hold values from 0 to 4095, each once within a row
- labels: int32 [4, 4096], P('rep'), may hold values 0 or 1
- proj: bfloat16 [64, 128, 32], replicated, may hold values from -0.5 to 0.5
- senet_in: float32 [64, 32], replicated, may hold values from -6 to 6
- senet_out: float32 [32, 64], replicated, may hold values from -1 to 1
- bilinear: float32 [32, 32], replicated, may hold values from -1 to 1
- w_first: bfloat16 [4096, 256], replicated, may hold values from -0.09375 to 0.09375
- w_second: bfloat16 [256, 256], replicated, may hold values from -0.75 to 0.75
- w_last: bfloat16 [256], replicated, may hold values from -0.375 to 0.375
Outputs:
- scores: float32 [4, 4096], P('rep', 'tab')
- d_pooled: bfloat16 [64, 16384, 128], P('tab', 'rep')
- d_proj: float32 [64, 128, 32], P('tab')
- d_senet_in: float32 [64, 32], replicated
- d_senet_out: float32 [32, 64], replicated
- d_bilinear: float32 [32, 32], replicated
- d_first: float32 [4096, 256], P('tab')
- d_second: float32 [256, 256], replicated
- d_last: float32 [256], replicated
Inputs may be any that keep to these rules, and one draw needn't show every extreme that they name: `widths`: each field's width is 128, 64, 32 or 16. `placement`: a permutation of the fields. `route`: each row is a permutation of 0 to 4095.
All inputs are finite; a program needn't handle non-finite values. No bound on the sum of `labels` on one device may be relied on, other than what follows from the above.
Results may differ from a plain program's by a relative error of at most 0.017.
Values may be sent and summed in bfloat16 or wider, within the bound.
A program may use at most 64 MiB of HBM per device.

v0:
```python
import jax
import jax.numpy as jnp
from jax import lax
from jax.sharding import PartitionSpec as P


def sent_to_all(value, axis):
    peers = lax.axis_size(axis)
    return lax.all_to_all(
        jnp.broadcast_to(value[None], (peers, *value.shape)), axis, 0, 0, tiled=True
    )


def of_everyone(value, axis):
    everything = sent_to_all(value, axis)
    return jnp.sum(everything.astype(jnp.float32), axis=0)


def laid_out(pieces, dim):
    lengths = list(pieces.shape[1:])
    lengths[dim] *= pieces.shape[0]
    return jnp.moveaxis(pieces, 0, dim).reshape(lengths)


def collect(value, axis, dim):
    pieces = sent_to_all(value, axis)
    return laid_out(pieces, dim)


def silu_slope(pre_act):
    logistic = jax.nn.sigmoid(pre_act)
    return logistic * (1.0 + pre_act * (1.0 - logistic))


def bilinear_forward(fields_in, bilinear, factor):
    product = jnp.einsum("fnc,cd->fnd", fields_in, bilinear)
    others = jnp.sum(fields_in, axis=0, keepdims=True) - fields_in
    return (product * others * factor, product, others)


def bilinear_backward(fields_in, product, others, upstream, bilinear, factor):
    d_product = upstream * others * factor
    d_others = upstream * product * factor
    d_fields = jnp.einsum("fnd,cd->fnc", d_product, bilinear)
    d_fields = d_fields + jnp.sum(d_others, axis=0, keepdims=True) - d_others
    d_weight = jnp.einsum("fnc,fnd->cd", fields_in, d_product)
    return (d_fields, d_weight)


def owner_pass(embeds, targets, senet_in, senet_out, bilinear, w_first, w_second, w_last):
    count = embeds.shape[0]
    width = embeds.shape[2]
    hidden = w_second.shape[0]
    factor = count ** (-0.5)
    first = w_first.reshape(2, count, width, hidden)
    dense = embeds.astype(jnp.float32)
    squeeze = jnp.mean(dense, axis=2)
    pre_one = jnp.einsum("fn,fr->rn", squeeze, senet_in)
    act_one = jax.nn.silu(pre_one)
    pre_two = jnp.einsum("rn,rf->fn", act_one, senet_out)
    weights = jax.nn.sigmoid(pre_two)
    scaled = weights[:, :, None] * dense
    plain_out, plain_prod, plain_rest = bilinear_forward(dense, bilinear, factor)
    scaled_out, scaled_prod, scaled_rest = bilinear_forward(scaled, bilinear, factor)
    joined = jnp.stack([plain_out, scaled_out]).astype(jnp.bfloat16)
    pre_hidden = jnp.einsum("kfnc,kfch->nh", joined, first, preferred_element_type=jnp.float32)
    hidden_one = jax.nn.silu(pre_hidden).astype(jnp.bfloat16)
    pre_second = jnp.dot(hidden_one, w_second, preferred_element_type=jnp.float32)
    hidden_two = jax.nn.silu(pre_second).astype(jnp.bfloat16)
    logits = jnp.dot(hidden_two, w_last, preferred_element_type=jnp.float32)
    grad_logit = jax.nn.sigmoid(logits) - targets
    d_last = jnp.dot(grad_logit, hidden_two.astype(jnp.float32))
    last_wide = w_last.astype(jnp.float32)
    d_pre_two = (grad_logit[:, None] * last_wide[None, :] * silu_slope(pre_second)).astype(
        jnp.bfloat16
    )
    d_second = jnp.dot(hidden_one.T, d_pre_two, preferred_element_type=jnp.float32)
    back_two = jnp.dot(d_pre_two, w_second.T, preferred_element_type=jnp.float32)
    d_pre_one = (back_two * silu_slope(pre_hidden)).astype(jnp.bfloat16)
    d_first = jnp.einsum(
        "kfnc,nh->kfch", joined, d_pre_one, preferred_element_type=jnp.float32
    ).reshape(-1, hidden)
    d_joined = jnp.einsum("nh,kfch->kfnc", d_pre_one, first, preferred_element_type=jnp.float32)
    d_plain, d_bil_plain = bilinear_backward(
        dense, plain_prod, plain_rest, d_joined[0], bilinear, factor
    )
    d_scaled, d_bil_scaled = bilinear_backward(
        scaled, scaled_prod, scaled_rest, d_joined[1], bilinear, factor
    )
    d_weights = jnp.sum(d_scaled * dense, axis=2)
    d_pre_w = d_weights * weights * (1.0 - weights)
    d_senet_out = jnp.einsum("rn,fn->rf", act_one, d_pre_w)
    d_act = jnp.einsum("fn,rf->rn", d_pre_w, senet_out) * silu_slope(pre_one)
    d_senet_in = jnp.einsum("fn,rn->fr", squeeze, d_act)
    d_squeeze = jnp.einsum("rn,fr->fn", d_act, senet_in)
    d_embeds = d_plain + weights[:, :, None] * d_scaled + d_squeeze[:, :, None] / width
    small = (d_senet_in, d_senet_out, d_bil_plain + d_bil_scaled, d_second, d_last)
    return (logits, d_embeds.astype(jnp.bfloat16), small, d_first, joined, d_pre_one)


def shards(
    pooled,
    widths,
    placement,
    route,
    labels,
    proj,
    senet_in,
    senet_out,
    bilinear,
    w_first,
    w_second,
    w_last,
):
    tab_count = lax.axis_size("tab")
    tab_index = lax.axis_index("tab")
    local_count = pooled.shape[0]
    rep_rows = pooled.shape[1]
    padded = pooled.shape[2]
    field_count = placement.shape[0]
    owner_rows = rep_rows // tab_count
    field_ids = jnp.arange(field_count, dtype=jnp.int32)
    matches = placement[:, None] == field_ids[None, :]
    slot_width = jnp.sum(jnp.where(matches, widths[None, :], 0), axis=1)
    slot_mask = (jnp.arange(padded, dtype=jnp.int32)[None, :] < slot_width[:, None]).astype(
        jnp.bfloat16
    )
    inverse = jnp.zeros_like(placement).at[placement].set(field_ids)
    targets = lax.dynamic_slice_in_dim(labels[0], tab_index * owner_rows, owner_rows).astype(
        jnp.float32
    )
    first_slot = tab_index * local_count
    local_fields = lax.dynamic_slice_in_dim(placement, first_slot, local_count)
    local_mask = lax.dynamic_slice_in_dim(slot_mask, first_slot, local_count, 0)
    local_proj = jnp.take(proj, local_fields, axis=0)
    masked = pooled * local_mask[:, None, :]
    embed_local = jnp.einsum(
        "fnc,fcd->fnd", masked, local_proj, preferred_element_type=jnp.float32
    ).astype(jnp.bfloat16)
    embed_slot = lax.all_to_all(embed_local, "tab", split_axis=1, concat_axis=0, tiled=True)
    logits, d_embeds, small, d_first_part, joined, d_pre_one = owner_pass(
        embed_slot[inverse], targets, senet_in, senet_out, bilinear, w_first, w_second, w_last
    )
    d_slot = d_embeds[placement]
    d_local = lax.all_to_all(d_slot, "tab", split_axis=0, concat_axis=1, tiled=True)
    back = jnp.einsum("fnd,fcd->fnc", d_local, local_proj, preferred_element_type=jnp.float32)
    back = (back * local_mask[:, None, :]).astype(jnp.bfloat16)
    d_proj_part = jnp.einsum("fnc,fnd->fcd", masked, d_local, preferred_element_type=jnp.float32)
    d_proj = of_everyone(d_proj_part.astype(jnp.bfloat16), "rep").astype(jnp.float32)
    first_tab = lax.psum_scatter(
        d_first_part.astype(jnp.bfloat16), "tab", scatter_dimension=0, tiled=True
    )
    d_first = of_everyone(first_tab, "rep").astype(jnp.float32)
    part_in, part_out, part_bil, part_second, part_last = small
    d_senet_in, d_senet_out, d_bilinear, d_second, d_last = lax.psum(
        (part_in, part_out, part_bil, part_second, part_last), ("tab", "rep")
    )
    all_logits = collect(logits, "tab", 0)
    wanted = lax.dynamic_slice_in_dim(route[0], tab_index * owner_rows, owner_rows)
    scores = jnp.take(all_logits, wanted)[None, :]
    return (scores, back, d_proj, d_senet_in, d_senet_out, d_bilinear, d_first, d_second, d_last)


def solution(mesh):
    placed = (
        P("tab", "rep", None),
        P(),
        P(),
        P("rep", None),
        P("rep", None),
        P(),
        P(),
        P(),
        P(),
        P(),
        P(),
        P(),
    )
    return jax.shard_map(
        shards,
        mesh=mesh,
        in_specs=placed,
        out_specs=(
            P("rep", "tab"),
            P("tab", "rep", None),
            P("tab", None, None),
            P(),
            P(),
            P(),
            P("tab", None),
            P(),
            P(),
        ),
        check_vma=False,
    )
```

profile of v0, /device:TPU:1, one launch (start us, length us, event | category | flops | bytes accessed | tf_op | source)
XLA Modules:
  0.0 225.5 jit_solution(7572727441180644628)
XLA Ops:
  9.9 1.6 gather_fusion
  11.5 2.4 %convolution_convert_fusion = bf16[2,4096,32]{1,2,0:T(8,128)(2,1)S(1)} fusion(bf16[2,4096,128]{2,1,0:T(8,128)(2,1)} %param.12, bf16[2,128]{1,0:T(2,128)(2,1)S(1)} %get-tuple-element.22, bf16[2,128,32]{1,2,0:T(8,128)(2,1)S(1)} %gather_fusion, pred[2]{0:T(512)(128)(4,1)S(1)} %get-tuple-element.17), kind=kOutput, calls=%fused_computation.7 | convolution fusion | flops 68427776 | bytes 2638338 | tf_op jit(solution)/shard_map/fnc,fcd->fnd/dot_general | solution.py:137
  14.0 3.8 %copy.56 = bf16[2,4096,32]{2,0,1:T(2,128)(2,1)} copy(bf16[2,4096,32]{1,2,0:T(8,128)(2,1)S(1)} %convolution_convert_fusion) | data formatting | bytes 1048576 | tf_op jit(solution)/shard_map/convert_element_type | solution.py:139
  17.8 5.9 %reshape.152 = bf16[32,2,4096]{2,1,0:T(2,128)(2,1)} reshape(bf16[4096,2,32]{2,1,0:T(2,128)(2,1)} %bitcast.166) | data formatting | bytes 1048576
  23.7 8.6 %all-to-all-start = ((bf16[32,2,4096]{2,1,0:T(2,128)(2,1)}), bf16[32,2,4096]{2,1,0:T(2,128)(2,1)S(1)}, u32[]{:S(2)}, u32[]{:S(2)}) async-start(bf16[32,2,4096]{2,1,0:T(2,128)(2,1)} %reshape.152), calls=%async_computation | async-start | bytes 1048576 | tf_op jit(solution)/shard_map/all_to_all | solution.py:140
  33.2 10.7 %all-to-all-done = bf16[32,2,4096]{2,1,0:T(2,128)(2,1)S(1)} async-done(((bf16[32,2,4096]{2,1,0:T(2,128)(2,1)}), bf16[32,2,4096]{2,1,0:T(2,128)(2,1)S(1)}, u32[]{:S(2)}, u32[]{:S(2)}) %all-to-all-start) | async-done | bytes 524320 | tf_op jit(solution)/shard_map/all_to_all | solution.py:140
  43.9 2.0 reshape.153
  45.8 4.7 %copy.73 = bf16[2,32,128,32]{2,3,0,1:T(8,128)(2,1)S(1)} copy(bf16[2,32,128,32]{3,0,2,1:T(2,128)(2,1)} %bitcast.167) | data formatting | bytes 1048576 | tf_op jit(solution)/shard_map/all_to_all | solution.py:140
  55.4 2.0 convolution_convert_fusion.1
  58.7 3.6 %all-to-all-start.1 = ((f32[32,1,128]{2,1,0:T(1,128)}), f32[32,1,128]{2,1,0:T(1,128)S(1)}, u32[]{:S(2)}, u32[]{:S(2)}) async-start(f32[32,1,128]{2,1,0:T(1,128)} %broadcast_in_dim.45), calls=%async_computation.1 | async-start | bytes 32768 | tf_op jit(solution)/shard_map/all_to_all | solution.py:9
  63.5 1.7 copy-done.3
  69.1 2.7 %fusion.14 = bf16[64,128,32]{1,2,0:T(8,128)(2,1)S(1)} fusion(f32[64,128,32]{1,2,0:T(8,128)} %get-tuple-element.28, bf16[64,128,32]{1,2,0:T(8,128)(2,1)S(1)} %gather_fusion.1, f32[2,64,128,32]{2,3,1,0:T(8,128)} %copy-done.1, f32[64,128]{1,0:T(8,128)S(1)} %fusion.24, f32[128,32]{0,1:T(8,128)S(1)} %get-tuple-element.9, f32[64,128]{1,0:T(8,128)S(1)} %fusion.28, ...), kind=kOutput, calls=%fused_computation.30 | convolution fusion | flops 19922944 | bytes 5345280 | tf_op jit(solution)/shard_map/fnd,cd->fnc/dot_general | solution.py:44
  73.2 7.4 %all-to-all-start.2 = ((bf16[64,128,32]{1,2,0:T(8,128)(2,1)}), bf16[64,128,32]{1,2,0:T(8,128)(2,1)S(1)}, u32[]{:S(2)}, u32[]{:S(2)}) async-start(bf16[64,128,32]{1,2,0:T(8,128)(2,1)} %gather_fusion.3), calls=%async_computation.2 | async-start | bytes 1048576 | tf_op jit(solution)/shard_map/all_to_all | solution.py:145
  80.7 1.6 fusion.34
  82.4 68.8 %all-reduce = (f32[64,32]{0,1:T(8,128)}, f32[32,64]{1,0:T(8,128)}, f32[32,32]{1,0:T(8,128)}, f32[256]{0:T(256)}) all-reduce(f32[64,32]{0,1:T(8,128)S(1)} %fusion.68, f32[32,64]{1,0:T(8,128)S(1)} %fusion.79, f32[32,32]{1,0:T(8,128)S(1)} %fusion.34, f32[256]{0:T(256)S(1)} %bitcast.171), channel_id=1, replica_groups=mesh['tab'=32,'rep'=4] {'tab','rep'}, use_global_device_ids=true, to_apply=%region_9.10 | all-reduce | flops 5376 | bytes 43008 | tf_op jit(solution)/shard_map/psum | solution.py:155
  152.4 2.2 fusion.29
  155.2 3.3 %all-to-all-start.3 = ((bf16[4,2,128,32]{2,3,1,0:T(8,128)(2,1)}), bf16[4,2,128,32]{2,3,1,0:T(8,128)(2,1)S(1)}, u32[]{:S(2)}, u32[]{:S(2)}) async-start(bf16[4,2,128,32]{2,3,1,0:T(8,128)(2,1)} %broadcast_in_dim.49), calls=%async_computation.3 | async-start | bytes 131072 | tf_op jit(solution)/shard_map/all_to_all | solution.py:9
  159.7 3.3 %all-to-all-done.3 = bf16[4,2,128,32]{2,3,1,0:T(8,128)(2,1)S(1)} async-done(((bf16[4,2,128,32]{2,3,1,0:T(8,128)(2,1)}), bf16[4,2,128,32]{2,3,1,0:T(8,128)(2,1)S(1)}, u32[]{:S(2)}, u32[]{:S(2)}) %all-to-all-start.3) | async-done | bytes 65568 | tf_op jit(solution)/shard_map/all_to_all | solution.py:9
  162.9 1.6 broadcast_in_dim.82
  164.5 3.4 %all-to-all-start.4 = ((bf16[4,128,256]{2,1,0:T(8,128)(2,1)}), bf16[4,128,256]{2,1,0:T(8,128)(2,1)S(1)}, u32[]{:S(2)}, u32[]{:S(2)}) async-start(bf16[4,128,256]{2,1,0:T(8,128)(2,1)} %broadcast_in_dim.82), calls=%async_computation.5 | async-start | bytes 524288 | tf_op jit(solution)/shard_map/all_to_all | solution.py:9
  167.9 2.3 %fusion = bf16[2,4096,128]{2,1,0:T(8,128)(2,1)} fusion(f32[2,128]{1,0:T(2,128)S(1)} %get-tuple-element.21, bf16[32,2,4,8,128]{4,3,2,1,0:T(8,128)(2,1)S(1)} %bitcast.170, bf16[2,128,32]{1,2,0:T(8,128)(2,1)S(1)} %gather_fusion, pred[2]{0:T(512)(128)(4,1)S(1)} %get-tuple-element.17), kind=kOutput, calls=%fused_computation.6 | convolution fusion | flops 69214208 | bytes 2638850 | tf_op jit(solution)/shard_map/fnd,fcd->fnc/dot_general | solution.py:146
  170.8 2.6 %all-to-all-done.4 = bf16[4,128,256]{2,1,0:T(8,128)(2,1)S(1)} async-done(((bf16[4,128,256]{2,1,0:T(8,128)(2,1)}), bf16[4,128,256]{2,1,0:T(8,128)(2,1)S(1)}, u32[]{:S(2)}, u32[]{:S(2)}) %all-to-all-start.4) | async-done | bytes 262176 | tf_op jit(solution)/shard_map/all_to_all | solution.py:9
  174.1 42.3 %all-reduce.3.cloned.1.call-done = f32[256,256]{1,0:T(8,128)} async-done(((f32[256,256]{1,0:T(8,128)}), f32[256,256]{1,0:T(8,128)}) %all-reduce.3.cloned.1.call-update) | async-done | bytes 262160 | tf_op jit(solution)/shard_map/psum | solution.py:155
  216.3 1.7 copy.92
  (74 shorter events, 19.6 us)
Async XLA Ops:
  8.0 45.2 %copy-start = (bf16[4096,256]{1,0:T(8,128)(2,1)S(1)}, bf16[4096,256]{1,0:T(8,128)(2,1)}, u32[]{:S(2)}) copy-start(bf16[4096,256]{1,0:T(8,128)(2,1)} %param.21) | copy-start | bytes 6291460
  17.8 14.5 %copy-start.11 = (bf16[256]{0:T(256)(128)(2,1)S(1)}, bf16[256]{0:T(256)(128)(2,1)}, u32[]{:S(2)}) copy-start(bf16[256]{0:T(256)(128)(2,1)} %param.23) | copy-start | bytes 1540
  17.8 14.5 %copy-start.8 = (s32[64]{0:T(128)S(1)}, s32[64]{0:T(128)}, u32[]{:S(2)}) copy-start(s32[64]{0:T(128)} %param.14) | copy-start | bytes 772
  23.7 20.2 %all-to-all-start = ((bf16[32,2,4096]{2,1,0:T(2,128)(2,1)}), bf16[32,2,4096]{2,1,0:T(2,128)(2,1)S(1)}, u32[]{:S(2)}, u32[]{:S(2)}) async-start(bf16[32,2,4096]{2,1,0:T(2,128)(2,1)} %reshape.152), calls=%async_computation | async-start | bytes 1048576 | tf_op jit(solution)/shard_map/all_to_all | solution.py:140
  32.3 130.7 %reduce-scatter.2.cloned.1.call-start = ((), (), s32[]{:S(2)}) async-start(), calls=%async_computation.6 | async-start | bytes 2162688 | tf_op jit(solution)/shard_map/reduce_scatter | solution.py:150
  50.5 0.8 copy-start.7
  50.5 1.0 copy-start.10
  50.5 1.3 copy-start.6
  52.2 1.0 copy-start.4
  52.6 1.2 copy-start.2
  53.2 0.9 copy-start.9
  58.7 14.5 %all-to-all-start.1 = ((f32[32,1,128]{2,1,0:T(1,128)}), f32[32,1,128]{2,1,0:T(1,128)S(1)}, u32[]{:S(2)}, u32[]{:S(2)}) async-start(f32[32,1,128]{2,1,0:T(1,128)} %broadcast_in_dim.45), calls=%async_computation.1 | async-start | bytes 32768 | tf_op jit(solution)/shard_map/all_to_all | solution.py:9
  62.4 154.0 %all-reduce.3.cloned.1.call-start = ((), (), s32[]{:S(2)}) async-start(), calls=%async_computation.7 | async-start | bytes 524288 | tf_op jit(solution)/shard_map/psum | solution.py:155
  63.1 2.8 %copy-start.1 = (f32[2,64,128,32]{2,3,1,0:T(8,128)}, f32[2,64,128,32]{2,3,1,0:T(8,128)S(1)}, u32[]{:S(2)}) copy-start(f32[2,64,128,32]{2,3,1,0:T(8,128)S(1)} %convolution_bitcast_fusion) | copy-start | bytes 6291460
  63.1 2.0 copy-start.3
  63.1 2.3 %copy-start.5 = (f32[64,128,32]{1,2,0:T(8,128)S(1)}, f32[64,128,32]{1,2,0:T(8,128)}, u32[]{:S(2)}) copy-start(f32[64,128,32]{1,2,0:T(8,128)} %copy-done.4) | copy-start | bytes 3145732
  73.2 79.1 %all-to-all-start.2 = ((bf16[64,128,32]{1,2,0:T(8,128)(2,1)}), bf16[64,128,32]{1,2,0:T(8,128)(2,1)S(1)}, u32[]{:S(2)}, u32[]{:S(2)}) async-start(bf16[64,128,32]{1,2,0:T(8,128)(2,1)} %gather_fusion.3), calls=%async_computation.2 | async-start | bytes 1048576 | tf_op jit(solution)/shard_map/all_to_all | solution.py:145
  155.2 7.7 %all-to-all-start.3 = ((bf16[4,2,128,32]{2,3,1,0:T(8,128)(2,1)}), bf16[4,2,128,32]{2,3,1,0:T(8,128)(2,1)S(1)}, u32[]{:S(2)}, u32[]{:S(2)}) async-start(bf16[4,2,128,32]{2,3,1,0:T(8,128)(2,1)} %broadcast_in_dim.49), calls=%async_computation.3 | async-start | bytes 131072 | tf_op jit(solution)/shard_map/all_to_all | solution.py:9
  164.5 8.9 %all-to-all-start.4 = ((bf16[4,128,256]{2,1,0:T(8,128)(2,1)}), bf16[4,128,256]{2,1,0:T(8,128)(2,1)S(1)}, u32[]{:S(2)}, u32[]{:S(2)}) async-start(bf16[4,128,256]{2,1,0:T(8,128)(2,1)} %broadcast_in_dim.82), calls=%async_computation.5 | async-start | bytes 524288 | tf_op jit(solution)/shard_map/all_to_all | solution.py:9
Sparse Core Ops, SparseCore 0:
  57.6 75.3 reduce-scatter.1
Sparse Core Ops, SparseCore 1:
  69.2 147.1 all-reduce.2
where the time goes:
time: 226 us; the launch traced here: 225 us
  blocking collectives  68.8 us (30%)
  waiting for transfers between devices  58.9 us (26%)
  local copies, waits for them, and re-layouts  29.1 us (13%)
  starting transfers between devices  26.4 us (12%)
  matrix products  20.3 us (9%)
  between operations  15.8 us (7%)
  other arithmetic  6.22 us (3%)
    psum x1, blocking collectives, shards(): lax.psum((part_in, part_out, part_bil, part_second, part_last), ('tab', '...  68.8 us
    psum x1, waiting for transfers between devices, shards(): lax.psum((part_in, part_out, part_bil, part_second, part_last), ('tab', '...  42.3 us
    unnamed x28, local copies, waits for them, and re-layouts  12.1 us
    all_to_all x1, waiting for transfers between devices, shards(): lax.all_to_all(embed_local, 'tab', split_axis=1, concat_axis=0, tiled=True)  10.7 us
    all_to_all x3, starting transfers between devices, sent_to_all(): lax.all_to_all(jnp.broadcast_to(value[None], (peers, *value.shape)), axis...  10.3 us
    all_to_all x1, starting transfers between devices, shards(): lax.all_to_all(embed_local, 'tab', split_axis=1, concat_axis=0, tiled=True)  8.58 us
    all_to_all x1, starting transfers between devices, shards(): lax.all_to_all(d_slot, 'tab', split_axis=0, concat_axis=1, tiled=True)  7.39 us
    all_to_all x3, waiting for transfers between devices, sent_to_all(): lax.all_to_all(jnp.broadcast_to(value[None], (peers, *value.shape)), axis...  5.88 us
  transfers between devices with their start and end apart: 7, of which 4 were waited for; matrix products, arithmetic and copies ran while one was open for 10% of the time, Pallas kernels for 0%

commit v1 on v0

--- a/solution.py
+++ b/solution.py
@@ -153,7 +153,7 @@
     d_first = of_everyone(first_tab, "rep").astype(jnp.float32)
     part_in, part_out, part_bil, part_second, part_last = small
     d_senet_in, d_senet_out, d_bilinear, d_second, d_last = lax.psum(
-        (part_in, part_out, part_bil, part_second, part_last), ("tab", "rep")
+        lax.psum((part_in, part_out, part_bil, part_second, part_last), "rep"), "tab"
     )
     all_logits = collect(logits, "tab", 0)
     wanted = lax.dynamic_slice_in_dim(route[0], tab_index * owner_rows, owner_rows)

time: 226 us -> 346 us (1.53)
  blocking collectives: 68.8 us -> 139 us
  waiting for transfers between devices: 58.9 us -> 108 us
    psum x1 -> x2, blocking collectives: 68.8 us -> 139 us  [the longest x1 123 us: shards(): lax.psum(lax.psum((part_in, part_out, part_bil, part_second, part_last),...]
    psum x1 -> x2, waiting for transfers between devices: 42.3 us -> 91.6 us  [the longest x1 91.6 us: shards(): lax.psum(lax.psum((part_in, part_out, part_bil, part_second, part_last),...]
    unnamed x28 -> x32, local copies, waits for them, and re-layouts: 12.1 us -> 10.8 us
  transfers between devices with their start and end apart: 7 -> 8, of which waited for: 4 -> 5; matrix products, arithmetic and copies ran while one was open for 10% -> 7% of each run, Pallas kernels for 0% -> 0%
where the time goes in v1:
time: 346 us; the launch traced here: 345 us
  blocking collectives  139 us (40%)
  waiting for transfers between devices  108 us (31%)
  local copies, waits for them, and re-layouts  27.8 us (8%)
  starting transfers between devices  25.9 us (7%)
  matrix products  19.6 us (6%)
  between operations  15.9 us (5%)
  other arithmetic  8.55 us (2%)
    psum x1, blocking collectives, shards(): lax.psum(lax.psum((part_in, part_out, part_bil, part_second, part_last),...  123 us
    psum x1, waiting for transfers between devices, shards(): lax.psum(lax.psum((part_in, part_out, part_bil, part_second, part_last),...  91.6 us
    psum x1, blocking collectives, shards(): lax.psum((part_in, part_out, part_bil, part_second, part_last), 'rep')  15.8 us
    unnamed x32, local copies, waits for them, and re-layouts  10.8 us
    all_to_all x3, starting transfers between devices, sent_to_all(): lax.all_to_all(jnp.broadcast_to(value[None], (peers, *value.shape)), axis...  10.3 us
    all_to_all x1, waiting for transfers between devices, shards(): lax.all_to_all(embed_local, 'tab', split_axis=1, concat_axis=0, tiled=True)  9.99 us
    all_to_all x1, starting transfers between devices, shards(): lax.all_to_all(embed_local, 'tab', split_axis=1, concat_axis=0, tiled=True)  8.58 us
  transfers between devices with their start and end apart: 8, of which 5 were waited for; matrix products, arithmetic and copies ran while one was open for 7% of the time, Pallas kernels for 0%

profile of v1, /device:TPU:1, one launch (start us, length us, event | category | flops | bytes accessed | tf_op | source)
XLA Modules:
  0.0 344.7 jit_solution(12666276388069028271)
XLA Ops:
  9.9 1.6 gather_fusion
  11.5 2.4 convolution_convert_fusion
  14.0 3.8 %copy.56 = bf16[2,4096,32]{2,0,1:T(2,128)(2,1)} copy(bf16[2,4096,32]{1,2,0:T(8,128)(2,1)S(1)} %convolution_convert_fusion) | data formatting | bytes 1048576 | tf_op jit(solution)/shard_map/convert_element_type | solution.py:139
  17.8 5.9 %reshape.152 = bf16[32,2,4096]{2,1,0:T(2,128)(2,1)} reshape(bf16[4096,2,32]{2,1,0:T(2,128)(2,1)} %bitcast.166) | data formatting | bytes 1048576
  23.7 8.6 %all-to-all-start = ((bf16[32,2,4096]{2,1,0:T(2,128)(2,1)}), bf16[32,2,4096]{2,1,0:T(2,128)(2,1)S(1)}, u32[]{:S(2)}, u32[]{:S(2)}) async-start(bf16[32,2,4096]{2,1,0:T(2,128)(2,1)} %reshape.152), calls=%async_computation | async-start | bytes 1048576 | tf_op jit(solution)/shard_map/all_to_all | solution.py:140
  33.9 10.0 %all-to-all-done = bf16[32,2,4096]{2,1,0:T(2,128)(2,1)S(1)} async-done(((bf16[32,2,4096]{2,1,0:T(2,128)(2,1)}), bf16[32,2,4096]{2,1,0:T(2,128)(2,1)S(1)}, u32[]{:S(2)}, u32[]{:S(2)}) %all-to-all-start) | async-done | bytes 524320 | tf_op jit(solution)/shard_map/all_to_all | solution.py:140
  43.9 2.0 reshape.153
  45.8 4.7 %copy.73 = bf16[2,32,128,32]{2,3,0,1:T(8,128)(2,1)S(1)} copy(bf16[2,32,128,32]{3,0,2,1:T(2,128)(2,1)} %bitcast.167) | data formatting | bytes 1048576 | tf_op jit(solution)/shard_map/all_to_all | solution.py:140
  56.5 3.1 convolution_convert_fusion.1
  59.6 2.0 convolution_bitcast_fusion
  62.3 3.6 %all-to-all-start.1 = ((f32[32,1,128]{2,1,0:T(1,128)}), f32[32,1,128]{2,1,0:T(1,128)S(1)}, u32[]{:S(2)}, u32[]{:S(2)}) async-start(f32[32,1,128]{2,1,0:T(1,128)} %broadcast_in_dim.45), calls=%async_computation.1 | async-start | bytes 32768 | tf_op jit(solution)/shard_map/all_to_all | solution.py:9
  65.9 2.9 fusion.66
  72.8 6.8 %all-to-all-start.2 = ((bf16[64,128,32]{1,2,0:T(8,128)(2,1)}), bf16[64,128,32]{1,2,0:T(8,128)(2,1)S(1)}, u32[]{:S(2)}, u32[]{:S(2)}) async-start(bf16[64,128,32]{1,2,0:T(8,128)(2,1)} %gather_fusion.3), calls=%async_computation.2 | async-start | bytes 1048576 | tf_op jit(solution)/shard_map/all_to_all | solution.py:145
  79.8 1.7 convolution_bitcast_fusion.1
  82.0 15.8 %all-reduce.1 = (f32[64,32]{0,1:T(8,128)S(1)}, f32[32,64]{1,0:T(8,128)S(1)}, f32[32,32]{1,0:T(8,128)S(1)}, f32[256]{0:T(256)S(1)}) all-reduce(f32[64,32]{0,1:T(8,128)S(1)} %fusion.68, f32[32,64]{1,0:T(8,128)S(1)} %fusion.79, f32[32,32]{1,0:T(8,128)S(1)} %fusion.34, f32[256]{0:T(256)S(1)} %bitcast.171), channel_id=1, replica_groups=mesh['tab'=32,'rep'=4] {'rep'}, use_global_device_ids=true, to_apply=%region_9.10 | all-reduce | flops 5376 | bytes 43008 | tf_op jit(solution)/shard_map/psum | solution.py:156
  97.9 123.2 %all-reduce = (f32[64,32]{0,1:T(8,128)}, f32[32,64]{1,0:T(8,128)}, f32[32,32]{1,0:T(8,128)}, f32[256]{0:T(256)}) all-reduce(f32[64,32]{0,1:T(8,128)S(1)} %get-tuple-element.17, f32[32,64]{1,0:T(8,128)S(1)} %get-tuple-element.18, f32[32,32]{1,0:T(8,128)S(1)} %get-tuple-element.19, ...), channel_id=1, replica_groups=mesh['tab'=32,'rep'=4] {'tab'}, use_global_device_ids=true, to_apply=%region_10.11 | all-reduce | flops 5376 | bytes 43008 | tf_op jit(solution)/shard_map/psum | solution.py:155
  222.3 2.1 fusion.29
  225.1 3.3 all-to-all-start.3
  229.6 3.2 all-to-all-done.3
  234.4 3.4 all-to-all-start.4
  237.8 2.3 fusion
  240.6 2.6 all-to-all-done.4
  243.9 91.6 %all-reduce.7.cloned.1.call-done = f32[256,256]{1,0:T(8,128)} async-done(((f32[256,256]{1,0:T(8,128)}), f32[256,256]{1,0:T(8,128)}) %all-reduce.7.cloned.1.call-update) | async-done | bytes 262160 | tf_op jit(solution)/shard_map/psum | solution.py:155
  335.6 1.7 copy.93
  (82 shorter events, 20.5 us)
Async XLA Ops:
  8.0 45.2 %copy-start = (bf16[4096,256]{1,0:T(8,128)(2,1)S(1)}, bf16[4096,256]{1,0:T(8,128)(2,1)}, u32[]{:S(2)}) copy-start(bf16[4096,256]{1,0:T(8,128)(2,1)} %param.21) | copy-start | bytes 6291460
  17.8 14.5 %copy-start.10 = (s32[64]{0:T(128)S(1)}, s32[64]{0:T(128)}, u32[]{:S(2)}) copy-start(s32[64]{0:T(128)} %param.14) | copy-start | bytes 772
  17.8 14.5 %copy-start.13 = (bf16[256]{0:T(256)(128)(2,1)S(1)}, bf16[256]{0:T(256)(128)(2,1)}, u32[]{:S(2)}) copy-start(bf16[256]{0:T(256)(128)(2,1)} %param.23) | copy-start | bytes 1540
  23.7 20.2 %all-to-all-start = ((bf16[32,2,4096]{2,1,0:T(2,128)(2,1)}), bf16[32,2,4096]{2,1,0:T(2,128)(2,1)S(1)}, u32[]{:S(2)}, u32[]{:S(2)}) async-start(bf16[32,2,4096]{2,1,0:T(2,128)(2,1)} %reshape.152), calls=%async_computation | async-start | bytes 1048576 | tf_op jit(solution)/shard_map/all_to_all | solution.py:140
  32.3 197.3 %all-reduce.5.cloned.1.call-start = ((), (), s32[]{:S(2)}) async-start(), calls=%async_computation.7 | async-start | bytes 524288 | tf_op jit(solution)/shard_map/psum | solution.py:156
  50.5 0.8 copy-start.9
  50.5 1.0 copy-start.12
  50.5 1.3 copy-start.8
  52.2 1.0 copy-start.5
  52.6 1.2 copy-start.3
  53.2 0.8 copy-start.7
  53.2 1.0 copy-start.11
  56.5 176.3 %reduce-scatter.2.cloned.1.call-start = ((), (), s32[]{:S(2)}) async-start(), calls=%async_computation.6 | async-start | bytes 2162688 | tf_op jit(solution)/shard_map/reduce_scatter | solution.py:150
  62.3 10.5 %all-to-all-start.1 = ((f32[32,1,128]{2,1,0:T(1,128)}), f32[32,1,128]{2,1,0:T(1,128)S(1)}, u32[]{:S(2)}, u32[]{:S(2)}) async-start(f32[32,1,128]{2,1,0:T(1,128)} %broadcast_in_dim.45), calls=%async_computation.1 | async-start | bytes 32768 | tf_op jit(solution)/shard_map/all_to_all | solution.py:9
  65.9 2.9 copy-start.1
  65.9 3.2 copy-start.6
  68.8 1.4 copy-start.4
  72.8 149.4 %all-to-all-start.2 = ((bf16[64,128,32]{1,2,0:T(8,128)(2,1)}), bf16[64,128,32]{1,2,0:T(8,128)(2,1)S(1)}, u32[]{:S(2)}, u32[]{:S(2)}) async-start(bf16[64,128,32]{1,2,0:T(8,128)(2,1)} %gather_fusion.3), calls=%async_computation.2 | async-start | bytes 1048576 | tf_op jit(solution)/shard_map/all_to_all | solution.py:145
  79.7 2.0 copy-start.2
  225.1 7.7 %all-to-all-start.3 = ((bf16[4,2,128,32]{2,3,1,0:T(8,128)(2,1)}), bf16[4,2,128,32]{2,3,1,0:T(8,128)(2,1)S(1)}, u32[]{:S(2)}, u32[]{:S(2)}) async-start(bf16[4,2,128,32]{2,3,1,0:T(8,128)(2,1)} %broadcast_in_dim.49), calls=%async_computation.3 | async-start | bytes 131072 | tf_op jit(solution)/shard_map/all_to_all | solution.py:9
  228.3 107.2 %all-reduce.7.cloned.1.call-start = ((), (), s32[]{:S(2)}) async-start(), calls=%async_computation.8 | async-start | bytes 524288 | tf_op jit(solution)/shard_map/psum | solution.py:155
  234.4 8.9 %all-to-all-start.4 = ((bf16[4,128,256]{2,1,0:T(8,128)(2,1)}), bf16[4,128,256]{2,1,0:T(8,128)(2,1)S(1)}, u32[]{:S(2)}, u32[]{:S(2)}) async-start(bf16[4,128,256]{2,1,0:T(8,128)(2,1)} %broadcast_in_dim.82), calls=%async_computation.5 | async-start | bytes 524288 | tf_op jit(solution)/shard_map/all_to_all | solution.py:9
Sparse Core Ops, SparseCore 0:
  56.6 38.5 all-reduce.4
Sparse Core Ops, SparseCore 1:
  60.5 75.2 reduce-scatter.1
  232.1 103.5 all-reduce.6
